TPU v7x, 32 devices: a whole 2x2x4 slice. The times are simulated.
32 devices in a mesh: groups: 2 (over x), rows: 16 (over z, y, core).
Axes of the slice: x: 2, y: 2, z: 4, core: 2. Of those that a mesh axis runs over, the one named last changes fastest.
Arguments:
- token_ids: int32 [1, 256], P(None, 'groups'), parts along dimension 1, may hold values from 0 to 32767
- parents: int32 [1, 8, 32], P(None, 'groups'), parts along dimension 1, may hold values from 0 to 31, as said below
- states: bfloat16 [256, 16, 128, 128], P(('groups', 'rows')), parts along dimension 0, may hold values from -1.75 to 1.75
- embed_table: bfloat16 [32768, 2048], P(None, 'rows'), may hold values from -6 to 6
- qkv_weight: bfloat16 [2048, 3, 2048], P(None, None, 'rows'), may hold values from -0.125 to 0.125
- gate_weight: float32 [16, 128], replicated, may hold values from -6 to 6
- gate_bias: float32 [16], replicated, may hold values from -2 to 3
- norm_gain: float32 [2048], replicated, may hold values from 0.1 to 1.9
- out_weight: bfloat16 [2048, 2048], P(None, 'rows'), may hold values from -0.125 to 0.125
Outputs:
- layer_out: bfloat16 [1, 256, 2048], P(None, 'groups', 'rows'), parts along dimension 1
- final_states: bfloat16 [256, 16, 128, 128], P(('groups', 'rows')), parts along dimension 0
There are 2 independent parts, one for each index of `groups`. A program takes and returns all parts, laid end to end along the dimension named above; an argument that names none is the same for every part. Nothing has to cross between parts.
Inputs may be any that keep to these rules, and one draw needn't show every extreme that they name: The 32 beams of a user fall into 4 aligned blocks of 8. In every step and for every user, at most 2 children of one block have parents in any one other block, and in every step some user has exactly 2 children of one block with parents in another block.
All inputs are finite; a program needn't handle non-finite values.
Results may differ from a plain program's by a relative error of at most 0.0074.
Values may be sent and summed in bfloat16 or wider, within the bound.
A program may use at most 64 MiB of HBM per device.

v0:
```python
import math
import jax
import jax.numpy as jnp
from jax import lax
from jax.sharding import PartitionSpec as P

CAP = 2


def from_partner(block, axis, stride):
    count = lax.axis_size(axis)
    route = []
    for low in range(count):
        high = low | 1 << stride
        if high != low and high < count:
            route += [(low, high), (high, low)]
    return lax.ppermute(block, axis, route)


def outgoing(state_now, parent_list, member, row_local, partner):
    target = jnp.bitwise_xor(member, partner)
    children = lax.dynamic_slice_in_dim(parent_list, target * row_local, row_local, 0)
    needed = children // row_local == member
    rank_index = jnp.cumsum(needed.astype(jnp.int32)) - 1
    slot_ids = jnp.arange(CAP, dtype=jnp.int32)
    chosen = jnp.sum(
        jnp.where(
            needed[None, :] & (rank_index[None, :] == slot_ids[:, None]),
            (children % row_local)[None, :],
            0,
        ),
        axis=1,
    )
    return jnp.take(state_now, chosen, axis=0)


def route(state_now, parent_list, member, row_local):
    first_out = outgoing(state_now, parent_list, member, row_local, 1)
    second_out = outgoing(state_now, parent_list, member, row_local, 2)
    corner_out = outgoing(state_now, parent_list, member, row_local, 3)
    got_one = from_partner(first_out, "rows", 0)
    got_two = from_partner(second_out, "rows", 1)
    relayed = from_partner(corner_out, "rows", 0)
    got_three = from_partner(relayed, "rows", 1)
    own_list = lax.dynamic_slice_in_dim(parent_list, member * row_local, row_local, 0)
    source = own_list // row_local
    partner = jnp.bitwise_xor(source, member)
    slot_index = jnp.arange(row_local, dtype=jnp.int32)
    earlier = (source[:, None] == source[None, :]) & (slot_index[:, None] > slot_index[None, :])
    rank_index = jnp.sum(earlier.astype(jnp.int32), axis=1)
    position = jnp.where(
        partner == 0, own_list % row_local, row_local + (partner - 1) * CAP + rank_index
    )
    pooled = jnp.concatenate([state_now, got_one, got_two, got_three], 0)
    return jnp.take(pooled, position, axis=0)


def per_device(
    token_ids,
    parents,
    states,
    embed_table,
    qkv_weight,
    gate_weight,
    gate_bias,
    norm_gain,
    out_weight,
):
    row_local = states.shape[0]
    heads = states.shape[1]
    head_size = states.shape[2]
    width = heads * head_size
    column_local = embed_table.shape[1]
    row_total = token_ids.shape[1]
    device = lax.axis_index("rows")
    member = device % 4
    user_index = device // 4
    weight_flat = qkv_weight.reshape(qkv_weight.shape[0], 3 * column_local)
    local_columns = jnp.take(embed_table, token_ids, axis=0)
    every_proj = jnp.einsum(
        "...rc,cf->...rf",
        lax.all_gather(local_columns, "rows", axis=2, tiled=True),
        weight_flat,
        preferred_element_type=jnp.float32,
    )
    state_now = states
    step_proj = every_proj[0]
    projected = step_proj.astype(jnp.bfloat16).reshape(row_total, 3, column_local)
    mine = lax.all_to_all(projected, "rows", split_axis=0, concat_axis=2, tiled=True)
    queries = mine[:, 0].reshape(row_local, heads, head_size)
    key_float = mine[:, 1].reshape(row_local, heads, head_size).astype(jnp.float32)
    values = mine[:, 2].reshape(row_local, heads, head_size).astype(jnp.float32)
    gate_logit = jnp.sum(key_float * gate_weight, axis=-1) / math.sqrt(head_size) + gate_bias
    decay_rate = jax.nn.sigmoid(gate_logit)
    key_unit = key_float * lax.rsqrt(jnp.sum(key_float * key_float, axis=-1, keepdims=True) + 1e-06)
    parent_list = lax.dynamic_index_in_dim(parents[0], user_index, 0, keepdims=False)
    prior_state = route(state_now, parent_list, member, row_local)
    new_state = (
        decay_rate[:, :, None, None] * prior_state.astype(jnp.float32)
        + key_unit[:, :, :, None] * values[:, :, None, :]
    )
    state_now = new_state.astype(jnp.bfloat16)
    readout = jnp.einsum("rhd,rhde->rhe", queries, state_now, preferred_element_type=jnp.float32)
    scaled = readout * lax.rsqrt(jnp.mean(readout * readout, axis=-1, keepdims=True) + 1e-05)
    normed = (scaled.reshape(row_local, width) * norm_gain).astype(jnp.bfloat16)
    attention = jnp.dot(
        lax.all_gather(normed, "rows", axis=0, tiled=True),
        out_weight,
        preferred_element_type=jnp.float32,
    )
    outputs = [(local_columns[0].astype(jnp.float32) + attention).astype(jnp.bfloat16)]
    return (jnp.stack(outputs), state_now)


def solution(mesh):
    placed = (
        P(None, "groups"),
        P(None, "groups", None),
        P(("groups", "rows"), None, None, None),
        P(None, "rows"),
        P(None, None, "rows"),
        P(),
        P(),
        P(),
        P(None, "rows"),
    )
    return jax.shard_map(
        per_device,
        mesh=mesh,
        in_specs=placed,
        out_specs=(P(None, "groups", "rows"), P(("groups", "rows"), None, None, None)),
        check_vma=False,
    )
```

profile of v0, /device:TPU:0, one launch (start us, length us, event | category | flops | bytes accessed | tf_op | source)
XLA Modules:
  0.0 127.5 jit_solution(7853263627772895128)
XLA Ops:
  0.7 0.9 compare_convert_fusion.2
  1.6 0.2 reduce-window.25
  1.8 0.1 fusion.16
  2.0 2.9 %gather_fusion.3 = bf16[2,16,128,128]{3,2,1,0:T(8,128)(2,1)S(1)} fusion(bf16[8,16,128,128]{3,2,1,0:T(8,128)(2,1)} %param.13, s32[1024]{0:T(1024)S(1)} %pad_clamp_fusion.2), kind=kCustom, calls=%fused_computation.1.clone | custom fusion | bytes 2097160 | tf_op jit(solution)/shard_map/jit(_take)/gather | solution.py:34
  4.9 1.1 broadcast_select_fusion.1
  6.1 3.0 %collective-permute-start.1 = (bf16[2,16,128,128]{3,2,1,0:T(8,128)(2,1)}, bf16[2,16,128,128]{3,2,1,0:T(8,128)(2,1)}, u32[]{:S(2)}, u32[]{:S(2)}) collective-permute-start(bf16[2,16,128,128]{3,2,1,0:T(8,128)(2,1)} %broadcast_select_fusion.1), channel_id=1, source_target_pairs={{0,2},{2,0},{1,3},{3,1},{4,6},{6,4},{5,7},{7,5},{8,10},{10,8},{9,1... | collective-permute-start | bytes 3145736 | tf_op jit(solution)/shard_map/ppermute | solution.py:17
  9.1 0.2 reduce-window.24
  9.3 0.1 fusion.15
  9.4 2.9 %gather_fusion.2 = bf16[2,16,128,128]{3,2,1,0:T(8,128)(2,1)S(1)} fusion(bf16[8,16,128,128]{3,2,1,0:T(8,128)(2,1)} %param.13, s32[1024]{0:T(1024)S(1)} %pad_clamp_fusion.3), kind=kCustom, calls=%fused_computation.clone | custom fusion | bytes 2097160 | tf_op jit(solution)/shard_map/jit(_take)/gather | solution.py:34
  12.4 1.2 broadcast_select_fusion.2
  13.6 0.2 reduce-window.26
  13.8 0.1 fusion.17
  13.9 2.9 %gather_fusion.4 = bf16[2,16,128,128]{3,2,1,0:T(8,128)(2,1)S(1)} fusion(bf16[8,16,128,128]{3,2,1,0:T(8,128)(2,1)} %param.13, s32[1024]{0:T(1024)S(1)} %pad_clamp_fusion.1), kind=kCustom, calls=%fused_computation.2.clone | custom fusion | bytes 2097160 | tf_op jit(solution)/shard_map/jit(_take)/gather | solution.py:34
  16.9 1.1 broadcast_select_fusion
  18.0 0.5 collective-permute-start.2
  18.6 5.1 %gather_fusion = bf16[128,128]{1,0:T(8,128)(2,1)S(1)} fusion(bf16[32768,128]{1,0:T(8,128)(2,1)} %param.14, s32[1024]{0:T(1024)S(1)} %pad_clamp_fusion.4), kind=kCustom, calls=%fused_computation.3 | custom fusion | bytes 66048 | tf_op jit(solution)/shard_map/jit(_take)/gather | solution.py:79
  23.8 26.1 %all_gather.6 = bf16[1,128,2048]{2,1,0:T(8,128)(2,1)S(1)} all-gather(bf16[1,128,128]{2,1,0:T(8,128)(2,1)S(1)} %bitcast_select_fusion), channel_id=1, replica_groups=mesh['groups'=2,'rows'=16] {'rows'}, dimensions={2}, use_global_device_ids=true | all-gather | bytes 557056 | tf_op jit(solution)/shard_map/all_gather | solution.py:82
  49.9 1.7 %copy.31 = bf16[2048,3,128]{0,2,1:T(8,128)(2,1)S(1)} copy(bf16[2048,3,128]{2,0,1:T(8,128)(2,1)} %param.15) | data formatting | bytes 3145728 | tf_op args[4]
  51.6 0.6 fusion.2
  52.2 0.7 copy.32
  52.9 3.5 %all-to-all-start = ((bf16[128,3,128]{2,1,0:T(4,128)(2,1)}), bf16[128,3,128]{2,1,0:T(4,128)(2,1)S(1)}, u32[]{:S(2)}, u32[]{:S(2)}) async-start(bf16[128,3,128]{2,1,0:T(4,128)(2,1)} %copy.32), calls=%async_computation | async-start | bytes 262144 | tf_op jit(solution)/shard_map/all_to_all | solution.py:89
  56.5 0.8 and_select_fusion.15
  57.2 0.2 convert_reduce_fusion
  57.5 1.9 %collective-permute-start.3 = (bf16[2,16,128,128]{3,2,1,0:T(8,128)(2,1)}, bf16[2,16,128,128]{3,2,1,0:T(8,128)(2,1)S(1)}, u32[]{:S(2)}, u32[]{:S(2)}) collective-permute-start(bf16[2,16,128,128]{3,2,1,0:T(8,128)(2,1)} %collective-permute-done.2), channel_id=1, source_target_pairs={{0,2},{2,0},{1,3},{3,1},{4,6},{6,4},{5,7},{7,5},{8,10},{10,8},{9,1... | collective-permute-start | bytes 3145736 | tf_op jit(solution)/shard_map/ppermute | solution.py:17
  59.3 5.0 %all-to-all-done = bf16[128,3,128]{2,1,0:T(4,128)(2,1)S(1)} async-done(((bf16[128,3,128]{2,1,0:T(4,128)(2,1)}), bf16[128,3,128]{2,1,0:T(4,128)(2,1)S(1)}, u32[]{:S(2)}, u32[]{:S(2)}) %all-to-all-start) | async-done | bytes 98336 | tf_op jit(solution)/shard_map/all_to_all | solution.py:89
  64.8 19.1 %collective-permute-done.3 = bf16[2,16,128,128]{3,2,1,0:T(8,128)(2,1)S(1)} collective-permute-done((bf16[2,16,128,128]{3,2,1,0:T(8,128)(2,1)}, bf16[2,16,128,128]{3,2,1,0:T(8,128)(2,1)S(1)}, u32[]{:S(2)}, u32[]{:S(2)}) %collective-permute-start.3) | collective-permute-done | bytes 1048608 | tf_op jit(solution)/shard_map/ppermute | solution.py:17
  84.0 8.1 %pad_maximum_fusion = bf16[14,16,128,128]{3,2,1,0:T(8,128)(2,1)} fusion(bf16[2,16,128,128]{3,2,1,0:T(8,128)(2,1)S(1)} %collective-permute-done.3, bf16[2,16,128,128]{3,2,1,0:T(8,128)(2,1)} %collective-permute-done.1, bf16[2,16,128,128]{3,2,1,0:T(8,128)(2,1)} %collective-permute-done, bf16[8,16,128,128]{3,2,1,0:T(8,128)(2,1)} %param.13), kind=kLoop, calls=%fused_computation.6 | loop fusion | flops 11010048 | bytes 14680064 | tf_op jit(solution)/shard_map/concatenate | solution.py:54
  92.0 6.2 %gather_fusion.1 = bf16[8,16,128,128]{3,2,1,0:T(8,128)(2,1)} fusion(bf16[14,16,128,128]{3,2,1,0:T(8,128)(2,1)} %pad_maximum_fusion, s32[1024]{0:T(1024)S(1)} %pad_clamp_fusion), kind=kCustom, calls=%fused_computation.4 | custom fusion | bytes 8388640 | tf_op jit(solution)/shard_map/jit(_take)/gather | solution.py:55
  98.2 4.6 %add_convert_fusion = bf16[8,16,128,128]{3,2,1,0:T(8,128)(2,1)S(1)} fusion(f32[8,16,128]{2,1,0:T(8,128)S(1)} %copy.36, f32[8,16,128]{2,1,0:T(8,128)S(1)} %copy.35, bf16[8,16,128,128]{3,2,1,0:T(8,128)(2,1)} %gather_fusion.1, f32[8,16]{1,0:T(8,128)S(1)} %add_divide_fusion, pred[8]{0:T(512)(128)(4,1)S(1)} %compare_and_fusion.3), kind=kLoop, calls=%fused_computation.5 | loop fusion | flops 12582912 | bytes 8520200 | tf_op jit(solution)/shard_map/convert_element_type | solution.py:102
  102.9 1.2 fusion.11
  104.3 22.2 %all_gather.7 = bf16[128,2048]{1,0:T(8,128)(2,1)S(1)} all-gather(bf16[8,2048]{1,0:T(8,128)(2,1)S(1)} %fusion.10), channel_id=1, replica_groups=mesh['groups'=2,'rows'=16] {'rows'}, dimensions={0}, use_global_device_ids=true | all-gather | bytes 557056 | tf_op jit(solution)/shard_map/all_gather | solution.py:107
  126.6 0.9 fusion.6
  (53 shorter events, 0.9 us)
Async XLA Ops:
  0.6 125.9 %copy-start = (bf16[2048,128]{1,0:T(8,128)(2,1)S(1)}, bf16[2048,128]{1,0:T(8,128)(2,1)}, u32[]{:S(2)}) copy-start(bf16[2048,128]{1,0:T(8,128)(2,1)} %param.19) | copy-start | bytes 1572868
  6.1 58.7 %collective-permute-start.1 = (bf16[2,16,128,128]{3,2,1,0:T(8,128)(2,1)}, bf16[2,16,128,128]{3,2,1,0:T(8,128)(2,1)}, u32[]{:S(2)}, u32[]{:S(2)}) collective-permute-start(bf16[2,16,128,128]{3,2,1,0:T(8,128)(2,1)} %broadcast_select_fusion.1), channel_id=1, source_target_pairs={{0,2},{2,0},{1,3},{3,1},{4,6},{6,4},{5,7},{7,5},{8,10},{10,8},{9,1... | collective-permute-start | bytes 3145736 | tf_op jit(solution)/shard_map/ppermute | solution.py:17
  9.4 9.1 %copy-start.5 = (s32[1,128]{1,0:T(1,128)S(1)}, s32[1,128]{1,0:T(1,128)}, u32[]{:S(2)}) copy-start(s32[1,128]{1,0:T(1,128)} %param.11) | copy-start | bytes 1540
  13.6 51.3 %collective-permute-start = (bf16[2,16,128,128]{3,2,1,0:T(8,128)(2,1)}, bf16[2,16,128,128]{3,2,1,0:T(8,128)(2,1)}, u32[]{:S(2)}, u32[]{:S(2)}) collective-permute-start(bf16[2,16,128,128]{3,2,1,0:T(8,128)(2,1)} %broadcast_select_fusion.2), channel_id=1, source_target_pairs={{0,1},{1,0},{2,3},{3,2},{4,5},{5,4},{6,7},{7,6},{8,9},{9,8},{10,11... | collective-permute-start | bytes 3145736 | tf_op jit(solution)/shard_map/ppermute | solution.py:17
  16.9 47.6 %copy-start.2 = (f32[16,128]{1,0:T(8,128)S(1)}, f32[16,128]{1,0:T(8,128)}, u32[]{:S(2)}) copy-start(f32[16,128]{1,0:T(8,128)} %param.16) | copy-start | bytes 24580
  18.0 46.8 %copy-start.4 = (f32[16]{0:T(128)S(1)}, f32[16]{0:T(128)}, u32[]{:S(2)}) copy-start(f32[16]{0:T(128)} %param.17) | copy-start | bytes 196
  18.0 39.4 %collective-permute-start.2 = (bf16[2,16,128,128]{3,2,1,0:T(8,128)(2,1)}, bf16[2,16,128,128]{3,2,1,0:T(8,128)(2,1)}, u32[]{:S(2)}, u32[]{:S(2)}) collective-permute-start(bf16[2,16,128,128]{3,2,1,0:T(8,128)(2,1)} %broadcast_select_fusion), channel_id=1, source_target_pairs={{0,1},{1,0},{2,3},{3,2},{4,5},{5,4},{6,7},{7,6},{8,9},{9,8},{10,11... | collective-permute-start | bytes 3145736 | tf_op jit(solution)/shard_map/ppermute | solution.py:17
  52.9 11.4 %all-to-all-start = ((bf16[128,3,128]{2,1,0:T(4,128)(2,1)}), bf16[128,3,128]{2,1,0:T(4,128)(2,1)S(1)}, u32[]{:S(2)}, u32[]{:S(2)}) async-start(bf16[128,3,128]{2,1,0:T(4,128)(2,1)} %copy.32), calls=%async_computation | async-start | bytes 262144 | tf_op jit(solution)/shard_map/all_to_all | solution.py:89
  57.5 26.5 %collective-permute-start.3 = (bf16[2,16,128,128]{3,2,1,0:T(8,128)(2,1)}, bf16[2,16,128,128]{3,2,1,0:T(8,128)(2,1)S(1)}, u32[]{:S(2)}, u32[]{:S(2)}) collective-permute-start(bf16[2,16,128,128]{3,2,1,0:T(8,128)(2,1)} %collective-permute-done.2), channel_id=1, source_target_pairs={{0,2},{2,0},{1,3},{3,1},{4,6},{6,4},{5,7},{7,5},{8,10},{10,8},{9,1... | collective-permute-start | bytes 3145736 | tf_op jit(solution)/shard_map/ppermute | solution.py:17
  102.9 24.6 %copy-start.1 = (bf16[8,16,128,128]{3,2,1,0:T(8,128)(2,1)}, bf16[8,16,128,128]{3,2,1,0:T(8,128)(2,1)S(1)}, u32[]{:S(2)}) copy-start(bf16[8,16,128,128]{3,2,1,0:T(8,128)(2,1)S(1)} %add_convert_fusion) | copy-start | bytes 12582916
  102.9 1.4 %copy-start.3 = (f32[2048]{0:T(1024)S(1)}, f32[2048]{0:T(1024)}, u32[]{:S(2)}) copy-start(f32[2048]{0:T(1024)} %param.18) | copy-start | bytes 24580
where the time goes:
time: 128 us; the launch traced here: 127 us
  blocking collectives  48.4 us (38%)
  waiting for transfers between devices  24.1 us (19%)
  local copies, waits for them, and re-layouts  22.8 us (18%)
  other arithmetic  19.6 us (15%)
  starting transfers between devices  8.87 us (7%)
  matrix products  2.7 us (2%)
    all_gather x1, blocking collectives, per_device(): lax.all_gather(local_columns, 'rows', axis=2, tiled=True)  26.1 us
    all_gather x1, blocking collectives, per_device(): lax.all_gather(normed, 'rows', axis=0, tiled=True)  22.2 us
    ppermute x4, waiting for transfers between devices, from_partner(): return lax.ppermute(block, axis, route)  19.2 us
    gather x3, local copies, waits for them, and re-layouts, outgoing(): return jnp.take(state_now, chosen, axis=0)  8.82 us
    concatenate x1, other arithmetic, route(): pooled = jnp.concatenate([state_now, got_one, got_two, got_three], 0)  8.06 us
    gather x1, local copies, waits for them, and re-layouts, route(): return jnp.take(pooled, position, axis=0)  6.18 us
    ppermute x4, starting transfers between devices, from_partner(): return lax.ppermute(block, axis, route)  5.36 us
    gather x1, local copies, waits for them, and re-layouts, per_device(): local_columns = jnp.take(embed_table, token_ids, axis=0)  5.11 us
  transfers between devices with their start and end apart: 5, of which 2 were waited for; matrix products, arithmetic and copies ran while one was open for 15% of the time, Pallas kernels for 0%

commit v1 on v0

--- a/solution.py
+++ b/solution.py
@@ -5,6 +5,27 @@
 from jax.sharding import PartitionSpec as P
 
 CAP = 2
+
+
+def gather_around(x, axis, dim):
+    size, position, rows = (lax.axis_size(axis), lax.axis_index(axis), x.shape[dim])
+    upward = [(i, (i + 1) % size) for i in range(size)]
+    behind = [(i, (i - 1) % size) for i in range(size)]
+    out = jnp.zeros((*x.shape[:dim], size * rows, *x.shape[dim + 1 :]), x.dtype)
+    out = lax.dynamic_update_slice_in_dim(out, x, position * rows, axis=dim)
+    from_left = from_right = x
+    half = size // 2
+    for hop in range(1, half + 1):
+        from_left = lax.ppermute(from_left, axis, upward)
+        out = lax.dynamic_update_slice_in_dim(
+            out, from_left, (position - hop) % size * rows, axis=dim
+        )
+        if hop < size - half:
+            from_right = lax.ppermute(from_right, axis, behind)
+            out = lax.dynamic_update_slice_in_dim(
+                out, from_right, (position + hop) % size * rows, axis=dim
+            )
+    return out
 
 
 def from_partner(block, axis, stride):
@@ -104,9 +125,7 @@
     scaled = readout * lax.rsqrt(jnp.mean(readout * readout, axis=-1, keepdims=True) + 1e-05)
     normed = (scaled.reshape(row_local, width) * norm_gain).astype(jnp.bfloat16)
     attention = jnp.dot(
-        lax.all_gather(normed, "rows", axis=0, tiled=True),
-        out_weight,
-        preferred_element_type=jnp.float32,
+        gather_around(normed, "rows", 0), out_weight, preferred_element_type=jnp.float32
     )
     outputs = [(local_columns[0].astype(jnp.float32) + attention).astype(jnp.bfloat16)]
     return (jnp.stack(outputs), state_now)

time: 128 us -> 156 us (1.22)
  starting transfers between devices: 8.87 us -> 40 us
  blocking collectives: 48.4 us -> 26.1 us
  waiting for transfers between devices: 24.1 us -> 41.3 us
  local copies, waits for them, and re-layouts: 22.8 us -> 24.9 us
    ppermute x0 -> x15, starting transfers between devices: none -> 31.1 us  [the longest x7 31.1 us: gather_around(): from_right = lax.ppermute(from_right, axis, behind)]
    all_gather x1 -> x0, blocking collectives: 22.2 us -> none  [per_device(): lax.all_gather(normed, 'rows', axis=0, tiled=True)]
    ppermute x0 -> x15, waiting for transfers between devices: none -> 17.2 us  [the longest x8 17.2 us: gather_around(): from_left = lax.ppermute(from_left, axis, upward)]
    unnamed x13, local copies, waits for them, and re-layouts: 1.76 us -> 3.75 us
  transfers between devices with their start and end apart: 5 -> 20, of which waited for: 2 -> 10; matrix products, arithmetic and copies ran while one was open for 15% -> 12% of each run, Pallas kernels for 0% -> 0%
where the time goes in v1:
time: 156 us
  waiting for transfers between devices  41.3 us (26%)
  starting transfers between devices  40 us (26%)
  blocking collectives  26.1 us (17%)
  local copies, waits for them, and re-layouts  24.9 us (16%)
  other arithmetic  19.6 us (13%)
  matrix products  2.69 us (2%)
    ppermute x7, starting transfers between devices, gather_around(): from_right = lax.ppermute(from_right, axis, behind)  31.1 us
    all_gather x1, blocking collectives, per_device(): lax.all_gather(local_columns, 'rows', axis=2, tiled=True)  26.1 us
    ppermute x4, waiting for transfers between devices, from_partner(): return lax.ppermute(block, axis, route)  19.2 us
    ppermute x8, waiting for transfers between devices, gather_around(): from_left = lax.ppermute(from_left, axis, upward)  17.2 us
    gather x3, local copies, waits for them, and re-layouts, outgoing(): return jnp.take(state_now, chosen, axis=0)  8.82 us
    concatenate x1, other arithmetic, route(): pooled = jnp.concatenate([state_now, got_one, got_two, got_three], 0)  8.11 us
    gather x1, local copies, waits for them, and re-layouts, route(): return jnp.take(pooled, position, axis=0)  6.18 us
    ppermute x4, starting transfers between devices, from_partner(): return lax.ppermute(block, axis, route)  5.36 us
  transfers between devices with their start and end apart: 20, of which 10 were waited for; matrix products, arithmetic and copies ran while one was open for 12% of the time, Pallas kernels for 0%

profile of v1, /device:TPU:0, one launch (start us, length us, event | category | flops | bytes accessed | tf_op | source)
XLA Modules:
  0.0 155.8 jit_solution(16505819087544585587)
XLA Ops:
  2.0 2.9 %gather_fusion.3 = bf16[2,16,128,128]{3,2,1,0:T(8,128)(2,1)S(1)} fusion(bf16[8,16,128,128]{3,2,1,0:T(8,128)(2,1)} %param.13, s32[1024]{0:T(1024)S(1)} %pad_clamp_fusion.2), kind=kCustom, calls=%fused_computation.1.clone | custom fusion | bytes 2097160 | tf_op jit(solution)/shard_map/jit(_take)/gather | solution.py:55
  6.0 3.0 %collective-permute-start.1 = (bf16[2,16,128,128]{3,2,1,0:T(8,128)(2,1)}, bf16[2,16,128,128]{3,2,1,0:T(8,128)(2,1)}, u32[]{:S(2)}, u32[]{:S(2)}) collective-permute-start(bf16[2,16,128,128]{3,2,1,0:T(8,128)(2,1)} %broadcast_select_fusion.1), channel_id=1, source_target_pairs={{0,2},{2,0},{1,3},{3,1},{4,6},{6,4},{5,7},{7,5},{8,10},{10,8},{9,1... | collective-permute-start | bytes 3145736 | tf_op jit(solution)/shard_map/ppermute | solution.py:38
  9.4 2.9 %gather_fusion.2 = bf16[2,16,128,128]{3,2,1,0:T(8,128)(2,1)S(1)} fusion(bf16[8,16,128,128]{3,2,1,0:T(8,128)(2,1)} %param.13, s32[1024]{0:T(1024)S(1)} %pad_clamp_fusion.3), kind=kCustom, calls=%fused_computation.clone | custom fusion | bytes 2097160 | tf_op jit(solution)/shard_map/jit(_take)/gather | solution.py:55
  12.3 1.2 broadcast_select_fusion.2
  13.9 2.9 %gather_fusion.4 = bf16[2,16,128,128]{3,2,1,0:T(8,128)(2,1)S(1)} fusion(bf16[8,16,128,128]{3,2,1,0:T(8,128)(2,1)} %param.13, s32[1024]{0:T(1024)S(1)} %pad_clamp_fusion.1), kind=kCustom, calls=%fused_computation.2.clone | custom fusion | bytes 2097160 | tf_op jit(solution)/shard_map/jit(_take)/gather | solution.py:55
  18.5 5.1 %gather_fusion = bf16[128,128]{1,0:T(8,128)(2,1)S(1)} fusion(bf16[32768,128]{1,0:T(8,128)(2,1)} %param.14, s32[1024]{0:T(1024)S(1)} %pad_clamp_fusion.4), kind=kCustom, calls=%fused_computation.3 | custom fusion | bytes 66048 | tf_op jit(solution)/shard_map/jit(_take)/gather | solution.py:100
  23.7 26.1 %all_gather.3 = bf16[1,128,2048]{2,1,0:T(8,128)(2,1)S(1)} all-gather(bf16[1,128,128]{2,1,0:T(8,128)(2,1)S(1)} %bitcast_select_fusion), channel_id=1, replica_groups=mesh['groups'=2,'rows'=16] {'rows'}, dimensions={2}, use_global_device_ids=true | all-gather | bytes 557056 | tf_op jit(solution)/shard_map/all_gather | solution.py:103
  49.9 1.7 %copy.31 = bf16[2048,3,128]{0,2,1:T(8,128)(2,1)S(1)} copy(bf16[2048,3,128]{2,0,1:T(8,128)(2,1)} %param.15) | data formatting | bytes 3145728 | tf_op args[4]
  52.9 3.5 %all-to-all-start = ((bf16[128,3,128]{2,1,0:T(4,128)(2,1)}), bf16[128,3,128]{2,1,0:T(4,128)(2,1)S(1)}, u32[]{:S(2)}, u32[]{:S(2)}) async-start(bf16[128,3,128]{2,1,0:T(4,128)(2,1)} %copy.32), calls=%async_computation | async-start | bytes 262144 | tf_op jit(solution)/shard_map/all_to_all | solution.py:110
  57.5 1.9 %collective-permute-start.3 = (bf16[2,16,128,128]{3,2,1,0:T(8,128)(2,1)}, bf16[2,16,128,128]{3,2,1,0:T(8,128)(2,1)S(1)}, u32[]{:S(2)}, u32[]{:S(2)}) collective-permute-start(bf16[2,16,128,128]{3,2,1,0:T(8,128)(2,1)} %collective-permute-done.2), channel_id=1, source_target_pairs={{0,2},{2,0},{1,3},{3,1},{4,6},{6,4},{5,7},{7,5},{8,10},{10,8},{9,1... | collective-permute-start | bytes 3145736 | tf_op jit(solution)/shard_map/ppermute | solution.py:38
  59.3 5.0 %all-to-all-done = bf16[128,3,128]{2,1,0:T(4,128)(2,1)S(1)} async-done(((bf16[128,3,128]{2,1,0:T(4,128)(2,1)}), bf16[128,3,128]{2,1,0:T(4,128)(2,1)S(1)}, u32[]{:S(2)}, u32[]{:S(2)}) %all-to-all-start) | async-done | bytes 98336 | tf_op jit(solution)/shard_map/all_to_all | solution.py:110
  64.8 19.1 %collective-permute-done.3 = bf16[2,16,128,128]{3,2,1,0:T(8,128)(2,1)S(1)} collective-permute-done((bf16[2,16,128,128]{3,2,1,0:T(8,128)(2,1)}, bf16[2,16,128,128]{3,2,1,0:T(8,128)(2,1)S(1)}, u32[]{:S(2)}, u32[]{:S(2)}) %collective-permute-start.3) | collective-permute-done | bytes 1048608 | tf_op jit(solution)/shard_map/ppermute | solution.py:38
  84.0 8.1 %pad_maximum_fusion = bf16[14,16,128,128]{3,2,1,0:T(8,128)(2,1)} fusion(bf16[2,16,128,128]{3,2,1,0:T(8,128)(2,1)S(1)} %collective-permute-done.3, bf16[2,16,128,128]{3,2,1,0:T(8,128)(2,1)} %collective-permute-done.1, bf16[2,16,128,128]{3,2,1,0:T(8,128)(2,1)} %collective-permute-done, bf16[8,16,128,128]{3,2,1,0:T(8,128)(2,1)} %param.13), kind=kLoop, calls=%fused_computation.6 | loop fusion | flops 11010048 | bytes 14680064 | tf_op jit(solution)/shard_map/concatenate | solution.py:75
  92.1 6.2 %gather_fusion.1 = bf16[8,16,128,128]{3,2,1,0:T(8,128)(2,1)} fusion(bf16[14,16,128,128]{3,2,1,0:T(8,128)(2,1)} %pad_maximum_fusion, s32[1024]{0:T(1024)S(1)} %pad_clamp_fusion), kind=kCustom, calls=%fused_computation.4 | custom fusion | bytes 8388640 | tf_op jit(solution)/shard_map/jit(_take)/gather | solution.py:76
  98.3 4.6 %add_convert_fusion = bf16[8,16,128,128]{3,2,1,0:T(8,128)(2,1)S(1)} fusion(f32[8,16,128]{2,1,0:T(8,128)S(1)} %copy.36, f32[8,16,128]{2,1,0:T(8,128)S(1)} %copy.35, bf16[8,16,128,128]{3,2,1,0:T(8,128)(2,1)} %gather_fusion.1, f32[8,16]{1,0:T(8,128)S(1)} %add_divide_fusion, pred[8]{0:T(512)(128)(4,1)S(1)} %compare_and_fusion.3), kind=kLoop, calls=%fused_computation.5 | loop fusion | flops 12582912 | bytes 8520200 | tf_op jit(solution)/shard_map/convert_element_type | solution.py:123
  102.9 2.0 %copy-done.1 = bf16[8,16,128,128]{3,2,1,0:T(8,128)(2,1)} copy-done((bf16[8,16,128,128]{3,2,1,0:T(8,128)(2,1)}, bf16[8,16,128,128]{3,2,1,0:T(8,128)(2,1)S(1)}, u32[]{:S(2)}) %copy-start.1) | copy-done | bytes 4194328
  104.9 1.2 fusion.12
  106.5 4.4 %collective-permute-start.5 = (bf16[8,2048]{1,0:T(8,128)(2,1)S(1)}, bf16[8,2048]{1,0:T(8,128)(2,1)S(1)}, u32[]{:S(2)}, u32[]{:S(2)}) collective-permute-start(bf16[8,2048]{1,0:T(8,128)(2,1)S(1)} %get-tuple-element.6), channel_id=1, source_target_pairs={{0,15},{1,0},{2,1},{3,2},{4,3},{5,4},{6,5},{7,6},{8,7},{9,8},{10,9... | collective-permute-start | bytes 98312 | tf_op jit(solution)/shard_map/ppermute | solution.py:24
  110.9 1.6 %collective-permute-done.4 = bf16[8,2048]{1,0:T(8,128)(2,1)S(1)} collective-permute-done((bf16[8,2048]{1,0:T(8,128)(2,1)S(1)}, bf16[8,2048]{1,0:T(8,128)(2,1)S(1)}, u32[]{:S(2)}, u32[]{:S(2)}) %collective-permute-start.4) | collective-permute-done | bytes 32800 | tf_op jit(solution)/shard_map/ppermute | solution.py:19
  112.5 4.4 %collective-permute-start.7 = (bf16[8,2048]{1,0:T(8,128)(2,1)S(1)}, bf16[8,2048]{1,0:T(8,128)(2,1)S(1)}, u32[]{:S(2)}, u32[]{:S(2)}) collective-permute-start(bf16[8,2048]{1,0:T(8,128)(2,1)S(1)} %collective-permute-done.5), channel_id=1, source_target_pairs={{0,15},{1,0},{2,1},{3,2},{4,3},{5,4},{6,5},{7,6},{8,7},{9,8},{10,9... | collective-permute-start | bytes 98312 | tf_op jit(solution)/shard_map/ppermute | solution.py:24
  116.9 1.7 %collective-permute-done.6 = bf16[8,2048]{1,0:T(8,128)(2,1)S(1)} collective-permute-done((bf16[8,2048]{1,0:T(8,128)(2,1)S(1)}, bf16[8,2048]{1,0:T(8,128)(2,1)S(1)}, u32[]{:S(2)}, u32[]{:S(2)}) %collective-permute-start.6) | collective-permute-done | bytes 32800 | tf_op jit(solution)/shard_map/ppermute | solution.py:19
  118.6 4.4 %collective-permute-start.9 = (bf16[8,2048]{1,0:T(8,128)(2,1)S(1)}, bf16[8,2048]{1,0:T(8,128)(2,1)S(1)}, u32[]{:S(2)}, u32[]{:S(2)}) collective-permute-start(bf16[8,2048]{1,0:T(8,128)(2,1)S(1)} %collective-permute-done.7), channel_id=1, source_target_pairs={{0,15},{1,0},{2,1},{3,2},{4,3},{5,4},{6,5},{7,6},{8,7},{9,8},{10,9... | collective-permute-start | bytes 98312 | tf_op jit(solution)/shard_map/ppermute | solution.py:24
  123.1 1.6 %collective-permute-done.8 = bf16[8,2048]{1,0:T(8,128)(2,1)S(1)} collective-permute-done((bf16[8,2048]{1,0:T(8,128)(2,1)S(1)}, bf16[8,2048]{1,0:T(8,128)(2,1)S(1)}, u32[]{:S(2)}, u32[]{:S(2)}) %collective-permute-start.8) | collective-permute-done | bytes 32800 | tf_op jit(solution)/shard_map/ppermute | solution.py:19
  124.7 4.4 %collective-permute-start.11 = (bf16[8,2048]{1,0:T(8,128)(2,1)S(1)}, bf16[8,2048]{1,0:T(8,128)(2,1)S(1)}, u32[]{:S(2)}, u32[]{:S(2)}) collective-permute-start(bf16[8,2048]{1,0:T(8,128)(2,1)S(1)} %collective-permute-done.9), channel_id=1, source_target_pairs={{0,15},{1,0},{2,1},{3,2},{4,3},{5,4},{6,5},{7,6},{8,7},{9,8},{10,9... | collective-permute-start | bytes 98312 | tf_op jit(solution)/shard_map/ppermute | solution.py:24
  129.1 1.6 %collective-permute-done.10 = bf16[8,2048]{1,0:T(8,128)(2,1)S(1)} collective-permute-done((bf16[8,2048]{1,0:T(8,128)(2,1)S(1)}, bf16[8,2048]{1,0:T(8,128)(2,1)S(1)}, u32[]{:S(2)}, u32[]{:S(2)}) %collective-permute-start.10) | collective-permute-done | bytes 32800 | tf_op jit(solution)/shard_map/ppermute | solution.py:19
  130.7 4.4 %collective-permute-start.13 = (bf16[8,2048]{1,0:T(8,128)(2,1)S(1)}, bf16[8,2048]{1,0:T(8,128)(2,1)S(1)}, u32[]{:S(2)}, u32[]{:S(2)}) collective-permute-start(bf16[8,2048]{1,0:T(8,128)(2,1)S(1)} %collective-permute-done.11), channel_id=1, source_target_pairs={{0,15},{1,0},{2,1},{3,2},{4,3},{5,4},{6,5},{7,6},{8,7},{9,8},{10,9... | collective-permute-start | bytes 98312 | tf_op jit(solution)/shard_map/ppermute | solution.py:24
  135.1 1.6 %collective-permute-done.12 = bf16[8,2048]{1,0:T(8,128)(2,1)S(1)} collective-permute-done((bf16[8,2048]{1,0:T(8,128)(2,1)S(1)}, bf16[8,2048]{1,0:T(8,128)(2,1)S(1)}, u32[]{:S(2)}, u32[]{:S(2)}) %collective-permute-start.12) | collective-permute-done | bytes 32800 | tf_op jit(solution)/shard_map/ppermute | solution.py:19
  136.7 4.4 %collective-permute-start.15 = (bf16[8,2048]{1,0:T(8,128)(2,1)S(1)}, bf16[8,2048]{1,0:T(8,128)(2,1)S(1)}, u32[]{:S(2)}, u32[]{:S(2)}) collective-permute-start(bf16[8,2048]{1,0:T(8,128)(2,1)S(1)} %collective-permute-done.13), channel_id=1, source_target_pairs={{0,15},{1,0},{2,1},{3,2},{4,3},{5,4},{6,5},{7,6},{8,7},{9,8},{10,9... | collective-permute-start | bytes 98312 | tf_op jit(solution)/shard_map/ppermute | solution.py:24
  141.2 1.6 %collective-permute-done.14 = bf16[8,2048]{1,0:T(8,128)(2,1)S(1)} collective-permute-done((bf16[8,2048]{1,0:T(8,128)(2,1)S(1)}, bf16[8,2048]{1,0:T(8,128)(2,1)S(1)}, u32[]{:S(2)}, u32[]{:S(2)}) %collective-permute-start.14) | collective-permute-done | bytes 32800 | tf_op jit(solution)/shard_map/ppermute | solution.py:19
  142.8 4.4 %collective-permute-start.17 = (bf16[8,2048]{1,0:T(8,128)(2,1)S(1)}, bf16[8,2048]{1,0:T(8,128)(2,1)S(1)}, u32[]{:S(2)}, u32[]{:S(2)}) collective-permute-start(bf16[8,2048]{1,0:T(8,128)(2,1)S(1)} %collective-permute-done.15), channel_id=1, source_target_pairs={{0,15},{1,0},{2,1},{3,2},{4,3},{5,4},{6,5},{7,6},{8,7},{9,8},{10,9... | collective-permute-start | bytes 98312 | tf_op jit(solution)/shard_map/ppermute | solution.py:24
  147.2 1.6 %collective-permute-done.16 = bf16[8,2048]{1,0:T(8,128)(2,1)S(1)} collective-permute-done((bf16[8,2048]{1,0:T(8,128)(2,1)S(1)}, bf16[8,2048]{1,0:T(8,128)(2,1)S(1)}, u32[]{:S(2)}, u32[]{:S(2)}) %collective-permute-start.16) | collective-permute-done | bytes 32800 | tf_op jit(solution)/shard_map/ppermute | solution.py:19
  148.8 6.0 %collective-permute-done.18 = bf16[8,2048]{1,0:T(8,128)(2,1)S(1)} collective-permute-done((bf16[8,2048]{1,0:T(8,128)(2,1)S(1)}, bf16[8,2048]{1,0:T(8,128)(2,1)S(1)}, u32[]{:S(2)}, u32[]{:S(2)}) %collective-permute-start.18) | collective-permute-done | bytes 32800 | tf_op jit(solution)/shard_map/ppermute | solution.py:19
  (97 shorter events, 8.9 us)
Async XLA Ops:
  0.6 154.2 %copy-start = (bf16[2048,128]{1,0:T(8,128)(2,1)S(1)}, bf16[2048,128]{1,0:T(8,128)(2,1)}, u32[]{:S(2)}) copy-start(bf16[2048,128]{1,0:T(8,128)(2,1)} %param.19) | copy-start | bytes 1572868
  6.0 58.8 %collective-permute-start.1 = (bf16[2,16,128,128]{3,2,1,0:T(8,128)(2,1)}, bf16[2,16,128,128]{3,2,1,0:T(8,128)(2,1)}, u32[]{:S(2)}, u32[]{:S(2)}) collective-permute-start(bf16[2,16,128,128]{3,2,1,0:T(8,128)(2,1)} %broadcast_select_fusion.1), channel_id=1, source_target_pairs={{0,2},{2,0},{1,3},{3,1},{4,6},{6,4},{5,7},{7,5},{8,10},{10,8},{9,1... | collective-permute-start | bytes 3145736 | tf_op jit(solution)/shard_map/ppermute | solution.py:38
  9.4 9.1 %copy-start.5 = (s32[1,128]{1,0:T(1,128)S(1)}, s32[1,128]{1,0:T(1,128)}, u32[]{:S(2)}) copy-start(s32[1,128]{1,0:T(1,128)} %param.11) | copy-start | bytes 1540
  13.5 51.3 %collective-permute-start = (bf16[2,16,128,128]{3,2,1,0:T(8,128)(2,1)}, bf16[2,16,128,128]{3,2,1,0:T(8,128)(2,1)}, u32[]{:S(2)}, u32[]{:S(2)}) collective-permute-start(bf16[2,16,128,128]{3,2,1,0:T(8,128)(2,1)} %broadcast_select_fusion.2), channel_id=1, source_target_pairs={{0,1},{1,0},{2,3},{3,2},{4,5},{5,4},{6,7},{7,6},{8,9},{9,8},{10,11... | collective-permute-start | bytes 3145736 | tf_op jit(solution)/shard_map/ppermute | solution.py:38
  16.8 47.6 %copy-start.2 = (f32[16,128]{1,0:T(8,128)S(1)}, f32[16,128]{1,0:T(8,128)}, u32[]{:S(2)}) copy-start(f32[16,128]{1,0:T(8,128)} %param.16) | copy-start | bytes 24580
  18.0 46.8 %copy-start.4 = (f32[16]{0:T(128)S(1)}, f32[16]{0:T(128)}, u32[]{:S(2)}) copy-start(f32[16]{0:T(128)} %param.17) | copy-start | bytes 196
  18.0 39.5 %collective-permute-start.2 = (bf16[2,16,128,128]{3,2,1,0:T(8,128)(2,1)}, bf16[2,16,128,128]{3,2,1,0:T(8,128)(2,1)}, u32[]{:S(2)}, u32[]{:S(2)}) collective-permute-start(bf16[2,16,128,128]{3,2,1,0:T(8,128)(2,1)} %broadcast_select_fusion), channel_id=1, source_target_pairs={{0,1},{1,0},{2,3},{3,2},{4,5},{5,4},{6,7},{7,6},{8,9},{9,8},{10,11... | collective-permute-start | bytes 3145736 | tf_op jit(solution)/shard_map/ppermute | solution.py:38
  52.9 11.4 %all-to-all-start = ((bf16[128,3,128]{2,1,0:T(4,128)(2,1)}), bf16[128,3,128]{2,1,0:T(4,128)(2,1)S(1)}, u32[]{:S(2)}, u32[]{:S(2)}) async-start(bf16[128,3,128]{2,1,0:T(4,128)(2,1)} %copy.32), calls=%async_computation | async-start | bytes 262144 | tf_op jit(solution)/shard_map/all_to_all | solution.py:110
  57.5 26.5 %collective-permute-start.3 = (bf16[2,16,128,128]{3,2,1,0:T(8,128)(2,1)}, bf16[2,16,128,128]{3,2,1,0:T(8,128)(2,1)S(1)}, u32[]{:S(2)}, u32[]{:S(2)}) collective-permute-start(bf16[2,16,128,128]{3,2,1,0:T(8,128)(2,1)} %collective-permute-done.2), channel_id=1, source_target_pairs={{0,2},{2,0},{1,3},{3,1},{4,6},{6,4},{5,7},{7,5},{8,10},{10,8},{9,1... | collective-permute-start | bytes 3145736 | tf_op jit(solution)/shard_map/ppermute | solution.py:38
  102.9 2.0 %copy-start.1 = (bf16[8,16,128,128]{3,2,1,0:T(8,128)(2,1)}, bf16[8,16,128,128]{3,2,1,0:T(8,128)(2,1)S(1)}, u32[]{:S(2)}) copy-start(bf16[8,16,128,128]{3,2,1,0:T(8,128)(2,1)S(1)} %add_convert_fusion) | copy-start | bytes 12582916
  102.9 3.4 %copy-start.3 = (f32[2048]{0:T(1024)S(1)}, f32[2048]{0:T(1024)}, u32[]{:S(2)}) copy-start(f32[2048]{0:T(1024)} %param.18) | copy-start | bytes 24580
  106.4 6.1 %collective-permute-start.4 = (bf16[8,2048]{1,0:T(8,128)(2,1)S(1)}, bf16[8,2048]{1,0:T(8,128)(2,1)S(1)}, u32[]{:S(2)}, u32[]{:S(2)}) collective-permute-start(bf16[8,2048]{1,0:T(8,128)(2,1)S(1)} %get-tuple-element.6), channel_id=1, source_target_pairs={{0,1},{1,2},{2,3},{3,4},{4,5},{5,6},{6,7},{7,8},{8,9},{9,10},{10,1... | collective-permute-start | bytes 98312 | tf_op jit(solution)/shard_map/ppermute | solution.py:19
  106.5 6.0 %collective-permute-start.5 = (bf16[8,2048]{1,0:T(8,128)(2,1)S(1)}, bf16[8,2048]{1,0:T(8,128)(2,1)S(1)}, u32[]{:S(2)}, u32[]{:S(2)}) collective-permute-start(bf16[8,2048]{1,0:T(8,128)(2,1)S(1)} %get-tuple-element.6), channel_id=1, source_target_pairs={{0,15},{1,0},{2,1},{3,2},{4,3},{5,4},{6,5},{7,6},{8,7},{9,8},{10,9... | collective-permute-start | bytes 98312 | tf_op jit(solution)/shard_map/ppermute | solution.py:24
  112.5 6.1 %collective-permute-start.6 = (bf16[8,2048]{1,0:T(8,128)(2,1)S(1)}, bf16[8,2048]{1,0:T(8,128)(2,1)S(1)}, u32[]{:S(2)}, u32[]{:S(2)}) collective-permute-start(bf16[8,2048]{1,0:T(8,128)(2,1)S(1)} %collective-permute-done.4), channel_id=1, source_target_pairs={{0,1},{1,2},{2,3},{3,4},{4,5},{5,6},{6,7},{7,8},{8,9},{9,10},{10,1... | collective-permute-start | bytes 98312 | tf_op jit(solution)/shard_map/ppermute | solution.py:19
  112.5 6.1 %collective-permute-start.7 = (bf16[8,2048]{1,0:T(8,128)(2,1)S(1)}, bf16[8,2048]{1,0:T(8,128)(2,1)S(1)}, u32[]{:S(2)}, u32[]{:S(2)}) collective-permute-start(bf16[8,2048]{1,0:T(8,128)(2,1)S(1)} %collective-permute-done.5), channel_id=1, source_target_pairs={{0,15},{1,0},{2,1},{3,2},{4,3},{5,4},{6,5},{7,6},{8,7},{9,8},{10,9... | collective-permute-start | bytes 98312 | tf_op jit(solution)/shard_map/ppermute | solution.py:24
  118.6 6.0 %collective-permute-start.8 = (bf16[8,2048]{1,0:T(8,128)(2,1)S(1)}, bf16[8,2048]{1,0:T(8,128)(2,1)S(1)}, u32[]{:S(2)}, u32[]{:S(2)}) collective-permute-start(bf16[8,2048]{1,0:T(8,128)(2,1)S(1)} %collective-permute-done.6), channel_id=1, source_target_pairs={{0,1},{1,2},{2,3},{3,4},{4,5},{5,6},{6,7},{7,8},{8,9},{9,10},{10,1... | collective-permute-start | bytes 98312 | tf_op jit(solution)/shard_map/ppermute | solution.py:19
  118.6 6.0 %collective-permute-start.9 = (bf16[8,2048]{1,0:T(8,128)(2,1)S(1)}, bf16[8,2048]{1,0:T(8,128)(2,1)S(1)}, u32[]{:S(2)}, u32[]{:S(2)}) collective-permute-start(bf16[8,2048]{1,0:T(8,128)(2,1)S(1)} %collective-permute-done.7), channel_id=1, source_target_pairs={{0,15},{1,0},{2,1},{3,2},{4,3},{5,4},{6,5},{7,6},{8,7},{9,8},{10,9... | collective-permute-start | bytes 98312 | tf_op jit(solution)/shard_map/ppermute | solution.py:24
  124.7 6.0 %collective-permute-start.10 = (bf16[8,2048]{1,0:T(8,128)(2,1)S(1)}, bf16[8,2048]{1,0:T(8,128)(2,1)S(1)}, u32[]{:S(2)}, u32[]{:S(2)}) collective-permute-start(bf16[8,2048]{1,0:T(8,128)(2,1)S(1)} %collective-permute-done.8), channel_id=1, source_target_pairs={{0,1},{1,2},{2,3},{3,4},{4,5},{5,6},{6,7},{7,8},{8,9},{9,10},{10,1... | collective-permute-start | bytes 98312 | tf_op jit(solution)/shard_map/ppermute | solution.py:19
  124.7 6.0 %collective-permute-start.11 = (bf16[8,2048]{1,0:T(8,128)(2,1)S(1)}, bf16[8,2048]{1,0:T(8,128)(2,1)S(1)}, u32[]{:S(2)}, u32[]{:S(2)}) collective-permute-start(bf16[8,2048]{1,0:T(8,128)(2,1)S(1)} %collective-permute-done.9), channel_id=1, source_target_pairs={{0,15},{1,0},{2,1},{3,2},{4,3},{5,4},{6,5},{7,6},{8,7},{9,8},{10,9... | collective-permute-start | bytes 98312 | tf_op jit(solution)/shard_map/ppermute | solution.py:24
  130.7 6.0 %collective-permute-start.12 = (bf16[8,2048]{1,0:T(8,128)(2,1)S(1)}, bf16[8,2048]{1,0:T(8,128)(2,1)S(1)}, u32[]{:S(2)}, u32[]{:S(2)}) collective-permute-start(bf16[8,2048]{1,0:T(8,128)(2,1)S(1)} %collective-permute-done.10), channel_id=1, source_target_pairs={{0,1},{1,2},{2,3},{3,4},{4,5},{5,6},{6,7},{7,8},{8,9},{9,10},{10,1... | collective-permute-start | bytes 98312 | tf_op jit(solution)/shard_map/ppermute | solution.py:19
  130.7 6.0 %collective-permute-start.13 = (bf16[8,2048]{1,0:T(8,128)(2,1)S(1)}, bf16[8,2048]{1,0:T(8,128)(2,1)S(1)}, u32[]{:S(2)}, u32[]{:S(2)}) collective-permute-start(bf16[8,2048]{1,0:T(8,128)(2,1)S(1)} %collective-permute-done.11), channel_id=1, source_target_pairs={{0,15},{1,0},{2,1},{3,2},{4,3},{5,4},{6,5},{7,6},{8,7},{9,8},{10,9... | collective-permute-start | bytes 98312 | tf_op jit(solution)/shard_map/ppermute | solution.py:24
  136.7 6.0 %collective-permute-start.14 = (bf16[8,2048]{1,0:T(8,128)(2,1)S(1)}, bf16[8,2048]{1,0:T(8,128)(2,1)S(1)}, u32[]{:S(2)}, u32[]{:S(2)}) collective-permute-start(bf16[8,2048]{1,0:T(8,128)(2,1)S(1)} %collective-permute-done.12), channel_id=1, source_target_pairs={{0,1},{1,2},{2,3},{3,4},{4,5},{5,6},{6,7},{7,8},{8,9},{9,10},{10,1... | collective-permute-start | bytes 98312 | tf_op jit(solution)/shard_map/ppermute | solution.py:19
  136.7 6.0 %collective-permute-start.15 = (bf16[8,2048]{1,0:T(8,128)(2,1)S(1)}, bf16[8,2048]{1,0:T(8,128)(2,1)S(1)}, u32[]{:S(2)}, u32[]{:S(2)}) collective-permute-start(bf16[8,2048]{1,0:T(8,128)(2,1)S(1)} %collective-permute-done.13), channel_id=1, source_target_pairs={{0,15},{1,0},{2,1},{3,2},{4,3},{5,4},{6,5},{7,6},{8,7},{9,8},{10,9... | collective-permute-start | bytes 98312 | tf_op jit(solution)/shard_map/ppermute | solution.py:24
  142.8 6.0 %collective-permute-start.16 = (bf16[8,2048]{1,0:T(8,128)(2,1)S(1)}, bf16[8,2048]{1,0:T(8,128)(2,1)S(1)}, u32[]{:S(2)}, u32[]{:S(2)}) collective-permute-start(bf16[8,2048]{1,0:T(8,128)(2,1)S(1)} %collective-permute-done.14), channel_id=1, source_target_pairs={{0,1},{1,2},{2,3},{3,4},{4,5},{5,6},{6,7},{7,8},{8,9},{9,10},{10,1... | collective-permute-start | bytes 98312 | tf_op jit(solution)/shard_map/ppermute | solution.py:19
  142.8 6.0 %collective-permute-start.17 = (bf16[8,2048]{1,0:T(8,128)(2,1)S(1)}, bf16[8,2048]{1,0:T(8,128)(2,1)S(1)}, u32[]{:S(2)}, u32[]{:S(2)}) collective-permute-start(bf16[8,2048]{1,0:T(8,128)(2,1)S(1)} %collective-permute-done.15), channel_id=1, source_target_pairs={{0,15},{1,0},{2,1},{3,2},{4,3},{5,4},{6,5},{7,6},{8,7},{9,8},{10,9... | collective-permute-start | bytes 98312 | tf_op jit(solution)/shard_map/ppermute | solution.py:24
  148.8 6.0 %collective-permute-start.18 = (bf16[8,2048]{1,0:T(8,128)(2,1)S(1)}, bf16[8,2048]{1,0:T(8,128)(2,1)S(1)}, u32[]{:S(2)}, u32[]{:S(2)}) collective-permute-start(bf16[8,2048]{1,0:T(8,128)(2,1)S(1)} %collective-permute-done.16), channel_id=1, source_target_pairs={{0,1},{1,2},{2,3},{3,4},{4,5},{5,6},{6,7},{7,8},{8,9},{9,10},{10,1... | collective-permute-start | bytes 98312 | tf_op jit(solution)/shard_map/ppermute | solution.py:19
